TPU v7x, 128 devices: a whole 4x4x4 slice. The times are simulated.
128 devices in a mesh: dp: 8 (over z, x_hi), ind: 16 (over y, x_lo, core).
Axes of the slice: x: 4 (x_hi: 2, x_lo: 2; x = x_hi * 2 + x_lo), y: 4, z: 4, core: 2. Of those that a mesh axis runs over, the one named last changes fastest.
Arguments:
- factor_rows: bfloat16 [8192, 8192], P('ind'), may hold values from -0.0625 to 0.0625
- diag_inverse: float32 [8192, 512], P('ind'), may hold values from -0.2 to 1.5, as said below
- inducing: float32 [8, 8192], P(None, 'ind'), may hold values from -6 to 6
- data_points: float32 [8, 2048], P(None, 'dp'), may hold values from -6 to 6
- lengthscale: float32 [8], replicated, may hold values from 1.5 to 4
- carried: float32 [8192, 2048], P('ind', 'dp'), may hold values from -4 to 4
- block_order: int32 [16], replicated, may hold values from 0 to 15, each once
- panel_pair: int32 [2], replicated, may hold values from 0 to 15, as said below
Outputs:
- solved: bfloat16 [8192, 2048], P('ind', 'dp')
- gram: float32 [1024, 1024], P('dp')
Inputs may be any that keep to these rules, and one draw needn't show every extreme that they name: `diag_inverse`: each 512 x 512 block is lower triangular with its diagonal between 0.5 and 1.5. `panel_pair`: the two positions differ, and one of them is the last position 15.
All inputs are finite; a program needn't handle non-finite values.
Results may differ from a plain program's by a relative error of at most 0.0095.
Values may be sent and summed in bfloat16 or wider, within the bound.
A program may use at most 64 MiB of HBM per device.

v0:
```python
import jax
import jax.numpy as jnp
from jax import lax
from jax.sharding import PartitionSpec as P


def from_root(block, axis, holder):
    block = jnp.where(lax.axis_index(axis) == holder, block, jnp.zeros_like(block))
    return lax.psum(block, axis)


def on_device(
    factor_rows, diag_inverse, inducing, data_points, lengthscale, carried, block_order, panel_pair
):
    owner_index = lax.axis_index("ind")
    width = diag_inverse.shape[1]
    slot_count = diag_inverse.shape[0] // width
    points = data_points.shape[1]
    block_count = block_order.shape[0]
    distance = jnp.zeros((slot_count * width, points), jnp.float32)
    for feature in range(inducing.shape[0]):
        offset = (inducing[feature][:, None] - data_points[feature][None, :]) / lengthscale[feature]
        distance = distance + offset * offset
    kernel = jnp.exp(-0.5 * distance)
    residual = (kernel - carried).reshape(slot_count, width, points)
    factor_slots = factor_rows.reshape(slot_count, width, block_count * width)
    inverse_slots = diag_inverse.reshape(slot_count, width, width)
    stored_ids = owner_index * slot_count + jnp.arange(slot_count, dtype=jnp.int32)
    positions = jnp.sum(
        jnp.where(
            block_order[None, :] == stored_ids[:, None],
            jnp.arange(block_count, dtype=jnp.int32)[None, :],
            0,
        ),
        axis=1,
    )

    def local_of(stored):
        return jnp.clip(stored - owner_index * slot_count, 0, slot_count - 1)

    def factor_cols(local_slot, index):
        return lax.dynamic_slice_in_dim(
            factor_slots[local_slot], (index * width).astype(jnp.int32), width, 1
        )

    def apply_inverse(local_slot, rows_now):
        return jnp.dot(
            inverse_slots[local_slot],
            rows_now,
            precision=lax.Precision.HIGHEST,
            preferred_element_type=jnp.float32,
        ).astype(jnp.bfloat16)

    def empty_panel():
        return jnp.zeros((width, points), jnp.bfloat16)

    def solve_own(residual, index):
        stored = block_order[index]
        local_slot = local_of(stored)

        def do_solve():
            return apply_inverse(local_slot, residual[local_slot])

        return (
            lax.cond(stored // slot_count == owner_index, do_solve, empty_panel),
            stored // slot_count,
        )

    def update_all(residual, panel_now, index):
        current = residual[0]
        cols_now = factor_cols(0, index)

        def do_update():
            return current - jnp.dot(cols_now, panel_now, preferred_element_type=jnp.float32)

        def keep_rows():
            return current

        updated = [lax.cond(positions[0] > index, do_update, keep_rows)]
        return jnp.stack(updated)

    def record(solved, first_tile, second_tile, panel_now, index):
        stored = block_order[index]
        local_slot = local_of(stored)
        placed = panel_now[None]
        solved = jnp.where(stored // slot_count == owner_index, placed, solved)
        first_tile = jnp.where(index == panel_pair[0], panel_now, first_tile)
        second_tile = jnp.where(index == panel_pair[1], panel_now, second_tile)
        return (solved, first_tile, second_tile)

    solved = jnp.zeros((slot_count, width, points), jnp.bfloat16)
    first_tile = empty_panel()
    second_tile = empty_panel()

    def turn(index, carry):
        residual, solved, first_tile, second_tile = carry
        own_panel, owner = solve_own(residual, index)
        panel_now = from_root(own_panel, "ind", owner)
        solved, first_tile, second_tile = record(solved, first_tile, second_tile, panel_now, index)
        residual = update_all(residual, panel_now, index)
        return (residual, solved, first_tile, second_tile)

    residual, solved, first_tile, second_tile = lax.fori_loop(
        0, block_count, turn, (residual, solved, first_tile, second_tile)
    )
    contract = (((1,), (1,)), ((), ()))
    upper_left = lax.dot_general(
        first_tile, first_tile, contract, preferred_element_type=jnp.float32
    )
    lower_left = lax.dot_general(
        second_tile, first_tile, contract, preferred_element_type=jnp.float32
    )
    lower_right = lax.dot_general(
        second_tile, second_tile, contract, preferred_element_type=jnp.float32
    )
    top_rows = jnp.concatenate([jnp.tril(upper_left), jnp.zeros_like(upper_left)], 1)
    bottom_rows = jnp.concatenate([lower_left, jnp.tril(lower_right)], 1)
    gram_tile = jnp.concatenate([top_rows, bottom_rows], 0)
    scale = 1.0 / (points * lax.axis_size("dp"))
    total = lax.psum(gram_tile.astype(jnp.bfloat16), "dp").astype(jnp.float32)
    share_rows = total.shape[0] // lax.axis_size("dp")
    gram = lax.dynamic_slice_in_dim(total, lax.axis_index("dp") * share_rows, share_rows, 0)
    return (solved.reshape(slot_count * width, points), gram * scale)


def solution(mesh):
    in_specs = (
        P("ind", None),
        P("ind", None),
        P(None, "ind"),
        P(None, "dp"),
        P(),
        P("ind", "dp"),
        P(),
        P(),
    )
    out_specs = (P("ind", "dp"), P("dp", None))
    return jax.shard_map(
        on_device, mesh=mesh, in_specs=in_specs, out_specs=out_specs, check_vma=False
    )
```

profile of v0, /device:TPU:1, one launch (start us, length us, event | category | flops | bytes accessed | tf_op | source)
XLA Modules:
  0.0 2139.1 jit_solution(13899003276891774317)
XLA Ops:
  8.0 1.6 fusion.13
  13.1 6.9 subtract_bitcast_fusion
  19.9 2000.2 %while.22 = (s32[]{:T(128)}, f32[1,512,256]{2,1,0:T(8,128)S(1)}, bf16[1,512,256]{2,1,0:T(8,128)(2,1)S(1)}, bf16[512,256]{1,0:T(8,128)(2,1)S(1)}, bf16[512,256]{1...) while((s32[]{:T(128)}, f32[1,512,256]{2,1,0:T(8,128)S(1)}, ...), condition=%wide.region_7.8_spmd.clone, body=%wide.region_1.7_spmd.clone.sunk | while | flops 940834816 | bytes 7864733 | solution.py:103
  26.8 119.0 %all-reduce.6.cloned.1.call-done = bf16[512,256]{1,0:T(8,128)(2,1)} async-done(((bf16[512,256]{1,0:T(8,128)(2,1)}), bf16[512,256]{1,0:T(8,128)(2,1)}) %all-reduce.6.cloned.1.call-update) | async-done | bytes 262160 | tf_op jit(solution)/shard_map/while/body/eval_jaxpr/psum | solution.py:9
  156.2 114.4 %all-reduce.6.cloned.1.call-done = bf16[512,256]{1,0:T(8,128)(2,1)} async-done(((bf16[512,256]{1,0:T(8,128)(2,1)}), bf16[512,256]{1,0:T(8,128)(2,1)}) %all-reduce.6.cloned.1.call-update) | async-done | bytes 262160 | tf_op jit(solution)/shard_map/while/body/eval_jaxpr/psum | solution.py:9
  281.0 114.4 %all-reduce.6.cloned.1.call-done = bf16[512,256]{1,0:T(8,128)(2,1)} async-done(((bf16[512,256]{1,0:T(8,128)(2,1)}), bf16[512,256]{1,0:T(8,128)(2,1)}) %all-reduce.6.cloned.1.call-update) | async-done | bytes 262160 | tf_op jit(solution)/shard_map/while/body/eval_jaxpr/psum | solution.py:9
  405.8 114.0 %all-reduce.6.cloned.1.call-done = bf16[512,256]{1,0:T(8,128)(2,1)} async-done(((bf16[512,256]{1,0:T(8,128)(2,1)}), bf16[512,256]{1,0:T(8,128)(2,1)}) %all-reduce.6.cloned.1.call-update) | async-done | bytes 262160 | tf_op jit(solution)/shard_map/while/body/eval_jaxpr/psum | solution.py:9
  530.3 114.1 %all-reduce.6.cloned.1.call-done = bf16[512,256]{1,0:T(8,128)(2,1)} async-done(((bf16[512,256]{1,0:T(8,128)(2,1)}), bf16[512,256]{1,0:T(8,128)(2,1)}) %all-reduce.6.cloned.1.call-update) | async-done | bytes 262160 | tf_op jit(solution)/shard_map/while/body/eval_jaxpr/psum | solution.py:9
  650.6 2.2 conditional.6
  650.6 2.2 convolution_convert_fusion
  657.0 112.4 %all-reduce.6.cloned.1.call-done = bf16[512,256]{1,0:T(8,128)(2,1)} async-done(((bf16[512,256]{1,0:T(8,128)(2,1)}), bf16[512,256]{1,0:T(8,128)(2,1)}) %all-reduce.6.cloned.1.call-update) | async-done | bytes 262160 | tf_op jit(solution)/shard_map/while/body/eval_jaxpr/psum | solution.py:9
  778.4 116.9 %all-reduce.6.cloned.1.call-done = bf16[512,256]{1,0:T(8,128)(2,1)} async-done(((bf16[512,256]{1,0:T(8,128)(2,1)}), bf16[512,256]{1,0:T(8,128)(2,1)}) %all-reduce.6.cloned.1.call-update) | async-done | bytes 262160 | tf_op jit(solution)/shard_map/while/body/eval_jaxpr/psum | solution.py:9
  904.3 115.8 %all-reduce.6.cloned.1.call-done = bf16[512,256]{1,0:T(8,128)(2,1)} async-done(((bf16[512,256]{1,0:T(8,128)(2,1)}), bf16[512,256]{1,0:T(8,128)(2,1)}) %all-reduce.6.cloned.1.call-update) | async-done | bytes 262160 | tf_op jit(solution)/shard_map/while/body/eval_jaxpr/psum | solution.py:9
  1029.1 115.8 %all-reduce.6.cloned.1.call-done = bf16[512,256]{1,0:T(8,128)(2,1)} async-done(((bf16[512,256]{1,0:T(8,128)(2,1)}), bf16[512,256]{1,0:T(8,128)(2,1)}) %all-reduce.6.cloned.1.call-update) | async-done | bytes 262160 | tf_op jit(solution)/shard_map/while/body/eval_jaxpr/psum | solution.py:9
  1153.9 115.3 %all-reduce.6.cloned.1.call-done = bf16[512,256]{1,0:T(8,128)(2,1)} async-done(((bf16[512,256]{1,0:T(8,128)(2,1)}), bf16[512,256]{1,0:T(8,128)(2,1)}) %all-reduce.6.cloned.1.call-update) | async-done | bytes 262160 | tf_op jit(solution)/shard_map/while/body/eval_jaxpr/psum | solution.py:9
  1278.2 116.7 %all-reduce.6.cloned.1.call-done = bf16[512,256]{1,0:T(8,128)(2,1)} async-done(((bf16[512,256]{1,0:T(8,128)(2,1)}), bf16[512,256]{1,0:T(8,128)(2,1)}) %all-reduce.6.cloned.1.call-update) | async-done | bytes 262160 | tf_op jit(solution)/shard_map/while/body/eval_jaxpr/psum | solution.py:9
  1403.9 115.5 %all-reduce.6.cloned.1.call-done = bf16[512,256]{1,0:T(8,128)(2,1)} async-done(((bf16[512,256]{1,0:T(8,128)(2,1)}), bf16[512,256]{1,0:T(8,128)(2,1)}) %all-reduce.6.cloned.1.call-update) | async-done | bytes 262160 | tf_op jit(solution)/shard_map/while/body/eval_jaxpr/psum | solution.py:9
  1528.4 115.8 %all-reduce.6.cloned.1.call-done = bf16[512,256]{1,0:T(8,128)(2,1)} async-done(((bf16[512,256]{1,0:T(8,128)(2,1)}), bf16[512,256]{1,0:T(8,128)(2,1)}) %all-reduce.6.cloned.1.call-update) | async-done | bytes 262160 | tf_op jit(solution)/shard_map/while/body/eval_jaxpr/psum | solution.py:9
  1653.2 115.5 %all-reduce.6.cloned.1.call-done = bf16[512,256]{1,0:T(8,128)(2,1)} async-done(((bf16[512,256]{1,0:T(8,128)(2,1)}), bf16[512,256]{1,0:T(8,128)(2,1)}) %all-reduce.6.cloned.1.call-update) | async-done | bytes 262160 | tf_op jit(solution)/shard_map/while/body/eval_jaxpr/psum | solution.py:9
  1777.7 115.8 %all-reduce.6.cloned.1.call-done = bf16[512,256]{1,0:T(8,128)(2,1)} async-done(((bf16[512,256]{1,0:T(8,128)(2,1)}), bf16[512,256]{1,0:T(8,128)(2,1)}) %all-reduce.6.cloned.1.call-update) | async-done | bytes 262160 | tf_op jit(solution)/shard_map/while/body/eval_jaxpr/psum | solution.py:9
  1902.5 115.5 %all-reduce.6.cloned.1.call-done = bf16[512,256]{1,0:T(8,128)(2,1)} async-done(((bf16[512,256]{1,0:T(8,128)(2,1)}), bf16[512,256]{1,0:T(8,128)(2,1)}) %all-reduce.6.cloned.1.call-update) | async-done | bytes 262160 | tf_op jit(solution)/shard_map/while/body/eval_jaxpr/psum | solution.py:9
  2021.2 1.6 fusion.6
  2022.8 107.3 %all-reduce.4.cloned.1.call-done = bf16[1024,1024]{1,0:T(8,128)(2,1)} async-done(((bf16[1024,1024]{1,0:T(8,128)(2,1)}), bf16[1024,1024]{1,0:T(8,128)(2,1)}) %all-reduce.4.cloned.1.call-update) | async-done | bytes 2097168 | tf_op jit(solution)/shard_map/psum | solution.py:120
  2130.2 1.8 convert_multiply_fusion
  (176 shorter events, 109.1 us)
Async XLA Ops:
  20.0 125.8 %all-reduce.6.cloned.1.call-start = ((), (), s32[]{:S(2)}) async-start(), calls=%async_computation.1 | async-start | bytes 524288 | tf_op jit(solution)/shard_map/while/body/eval_jaxpr/psum | solution.py:9
  149.4 121.2 %all-reduce.6.cloned.1.call-start = ((), (), s32[]{:S(2)}) async-start(), calls=%async_computation.1 | async-start | bytes 524288 | tf_op jit(solution)/shard_map/while/body/eval_jaxpr/psum | solution.py:9
  274.2 121.2 %all-reduce.6.cloned.1.call-start = ((), (), s32[]{:S(2)}) async-start(), calls=%async_computation.1 | async-start | bytes 524288 | tf_op jit(solution)/shard_map/while/body/eval_jaxpr/psum | solution.py:9
  399.0 120.9 %all-reduce.6.cloned.1.call-start = ((), (), s32[]{:S(2)}) async-start(), calls=%async_computation.1 | async-start | bytes 524288 | tf_op jit(solution)/shard_map/while/body/eval_jaxpr/psum | solution.py:9
  523.5 120.9 %all-reduce.6.cloned.1.call-start = ((), (), s32[]{:S(2)}) async-start(), calls=%async_computation.1 | async-start | bytes 524288 | tf_op jit(solution)/shard_map/while/body/eval_jaxpr/psum | solution.py:9
  648.0 121.4 %all-reduce.6.cloned.1.call-start = ((), (), s32[]{:S(2)}) async-start(), calls=%async_computation.1 | async-start | bytes 524288 | tf_op jit(solution)/shard_map/while/body/eval_jaxpr/psum | solution.py:9
  771.6 123.7 %all-reduce.6.cloned.1.call-start = ((), (), s32[]{:S(2)}) async-start(), calls=%async_computation.1 | async-start | bytes 524288 | tf_op jit(solution)/shard_map/while/body/eval_jaxpr/psum | solution.py:9
  897.4 122.6 %all-reduce.6.cloned.1.call-start = ((), (), s32[]{:S(2)}) async-start(), calls=%async_computation.1 | async-start | bytes 524288 | tf_op jit(solution)/shard_map/while/body/eval_jaxpr/psum | solution.py:9
  1022.3 122.6 %all-reduce.6.cloned.1.call-start = ((), (), s32[]{:S(2)}) async-start(), calls=%async_computation.1 | async-start | bytes 524288 | tf_op jit(solution)/shard_map/while/body/eval_jaxpr/psum | solution.py:9
  1147.1 122.1 %all-reduce.6.cloned.1.call-start = ((), (), s32[]{:S(2)}) async-start(), calls=%async_computation.1 | async-start | bytes 524288 | tf_op jit(solution)/shard_map/while/body/eval_jaxpr/psum | solution.py:9
  1271.4 123.5 %all-reduce.6.cloned.1.call-start = ((), (), s32[]{:S(2)}) async-start(), calls=%async_computation.1 | async-start | bytes 524288 | tf_op jit(solution)/shard_map/while/body/eval_jaxpr/psum | solution.py:9
  1397.1 122.3 %all-reduce.6.cloned.1.call-start = ((), (), s32[]{:S(2)}) async-start(), calls=%async_computation.1 | async-start | bytes 524288 | tf_op jit(solution)/shard_map/while/body/eval_jaxpr/psum | solution.py:9
  1521.6 122.6 %all-reduce.6.cloned.1.call-start = ((), (), s32[]{:S(2)}) async-start(), calls=%async_computation.1 | async-start | bytes 524288 | tf_op jit(solution)/shard_map/while/body/eval_jaxpr/psum | solution.py:9
  1646.4 122.3 %all-reduce.6.cloned.1.call-start = ((), (), s32[]{:S(2)}) async-start(), calls=%async_computation.1 | async-start | bytes 524288 | tf_op jit(solution)/shard_map/while/body/eval_jaxpr/psum | solution.py:9
  1770.9 122.6 %all-reduce.6.cloned.1.call-start = ((), (), s32[]{:S(2)}) async-start(), calls=%async_computation.1 | async-start | bytes 524288 | tf_op jit(solution)/shard_map/while/body/eval_jaxpr/psum | solution.py:9
  1895.7 122.3 %all-reduce.6.cloned.1.call-start = ((), (), s32[]{:S(2)}) async-start(), calls=%async_computation.1 | async-start | bytes 524288 | tf_op jit(solution)/shard_map/while/body/eval_jaxpr/psum | solution.py:9
  2020.1 2.7 copy-start
  2020.2 110.0 %all-reduce.4.cloned.1.call-start = ((), (), s32[]{:S(2)}) async-start(), calls=%async_computation | async-start | bytes 4194304 | tf_op jit(solution)/shard_map/psum | solution.py:120
Sparse Core Ops, SparseCore 0:
  23.8 121.9 all-reduce.5
  153.2 117.2 all-reduce.5
  278.0 117.2 all-reduce.5
  402.5 117.2 all-reduce.5
  527.0 117.2 all-reduce.5
  653.7 115.6 all-reduce.5
  775.4 119.7 all-reduce.5
  901.3 118.7 all-reduce.5
  1026.1 118.7 all-reduce.5
  1150.6 118.5 all-reduce.5
  1275.2 119.6 all-reduce.5
  1400.6 118.7 all-reduce.5
  1525.4 118.7 all-reduce.5
  1649.9 118.7 all-reduce.5
  1774.4 118.9 all-reduce.5
  1899.2 118.7 all-reduce.5
Sparse Core Ops, SparseCore 1:
  2023.2 106.9 all-reduce.3
where the time goes:
time: 2150 us; the launch traced here: 2140 us
  waiting for transfers between devices  1950 us (91%)
  other arithmetic  58.1 us (3%)
  loops' own time  54.4 us (3%)
  local copies, waits for them, and re-layouts  46.2 us (2%)
    psum x16, waiting for transfers between devices, from_root(): return lax.psum(block, axis)  1850 us
    psum x1, waiting for transfers between devices, on_device(): total = lax.psum(gram_tile.astype(jnp.bfloat16), 'dp').astype(jnp.float32)  107 us
    another operation x1, loops' own time, on_device(): lax.fori_loop(0, block_count, turn, (residual, solved, first_tile, second...  54.1 us
  transfers between devices with their start and end apart: 17, of which 17 were waited for; matrix products, arithmetic and copies ran while one was open for 1% of the time, Pallas kernels for 0%

commit v1 on v0

v1 whole, which is shorter than its diff:
```python
import functools

import jax
import jax.numpy as jnp
from jax import lax
from jax.experimental import pallas as pl
from jax.experimental.pallas import tpu as pltpu
from jax.sharding import PartitionSpec as P

MESH = pl.DeviceIdType.MESH
NT = (((1,), (1,)), ((), ()))
TN = (((0,), (0,)), ((), ()))
f32 = jnp.float32
bf16 = jnp.bfloat16

NB, W, NODES, QUAD = 16, 512, 4, 4


def kernel(
    order, pair, scales, factor, dinv, ind_t, points, carried, solved_t, gram,
    stage, fact, ycur, y0t, cand, xall, fcrit, dbf, xq, solt, st, parts, inbox, piece, tile,
    n_sem, y_s, y_r, f_s, f_r, l_s, l_r, c_s, c_r, s_s, s_r, g_s, g_r, o_s, o_r,
):
    cols = points.shape[1]
    share = cols // QUAD
    half = share // 2
    dp = lax.axis_index("dp")
    me = lax.axis_index("ind")
    node = lax.div(me, QUAD)
    q = lax.rem(me, QUAD)
    core = lax.rem(q, 2)
    xlo = lax.div(q, 2)
    q1 = 2 * xlo + 1 - core
    q2 = 2 * (1 - xlo) + core
    q3 = 2 * (1 - xlo) + 1 - core
    base = node * QUAD
    up = lax.rem(node + 1, NODES) * QUAD + q
    down = lax.rem(node + NODES - 1, NODES) * QUAD + q
    other_dp = dp + 1 - 2 * lax.rem(dp, 2)
    rank = dp * QUAD + q
    ranks = 8 * QUAD

    def at(d, i):
        return {"dp": d, "ind": i}

    def remote(src, dst, ssem, rsem, dev):
        return pltpu.make_async_remote_copy(
            src_ref=src, dst_ref=dst, send_sem=ssem, recv_sem=rsem,
            device_id=dev, device_id_type=MESH,
        )

    def n_copy(b):
        return pltpu.make_async_copy(
            factor.at[:, pl.ds(pl.multiple_of(b * W, W), W)], stage.at[b], n_sem.at[b]
        )

    @pl.loop(0, NB - 1)
    def _(b):
        n_copy(b).start()

    barrier = pltpu.get_barrier_semaphore()

    @pl.loop(1, ranks)
    def _(k):
        t = lax.rem(rank + k, ranks)
        pl.semaphore_signal(
            barrier, inc=1, device_id=at(lax.div(t, QUAD), base + lax.rem(t, QUAD)), device_id_type=MESH
        )

    @pl.loop(0, NB - QUAD)
    def _(k):
        pl.semaphore_signal(
            barrier, inc=1, device_id=at(dp, lax.rem(base + QUAD + k, NB)), device_id_type=MESH
        )

    distance = jnp.zeros((W, cols), f32)
    for feature in range(points.shape[0]):
        inverse = jnp.full((1, 1), 1.0, f32) / scales[feature]
        offset = (ind_t[:, feature : feature + 1] - points[feature : feature + 1, :]) * inverse
        distance = distance + offset * offset
    residual = jnp.exp(-0.5 * distance) - carried[...]
    y0 = jnp.dot(dinv[...], residual, precision=lax.Precision.HIGHEST, preferred_element_type=f32)
    y0t[...] = y0.T
    dbf[...] = dinv[...].astype(bf16)

    pl.semaphore_wait(barrier, ranks - 1 + NB - QUAD)

    quad = (q2, q3, q1)

    def y_copy(k):
        to = quad[k]
        return remote(
            y0t.at[pl.ds(pl.multiple_of(to * share, share), share)], ycur.at[q],
            y_s.at[k], y_r.at[k], at(dp, base + to),
        )

    for k in range(3):
        y_copy(k).start()
    ycur[q] = y0t[pl.ds(pl.multiple_of(q * share, share), share), :]

    top, bottom = pl.ds(0, W // 2), pl.ds(W // 2, W // 2)

    def f_copies(b):
        return (
            remote(fact.at[b, q, top], fact.at[b, q, top], f_s.at[b, 0], f_r.at[b, 0], at(dp, base + q2)),
            remote(fact.at[b, q, bottom], fact.at[b, q, bottom], f_s.at[b, 1], f_r.at[b, 1], at(other_dp, base + q2)),
            remote(fact.at[b, q], fact.at[b, q], f_s.at[b, 2], f_r.at[b, 2], at(dp, base + q1)),
        )

    def relay(b):
        return remote(fact.at[b, q2], fact.at[b, q2], l_s.at[b], l_r.at[b], at(dp, base + q1))

    @pl.loop(0, NB - 1)
    def _(b):
        n_copy(b).wait()
        fact[b, q] = jnp.dot(dbf[...], stage[b], preferred_element_type=f32).astype(bf16)
        for copy in f_copies(b):
            copy.start()

    def c_first(b):
        return (
            remote(cand.at[b, 0], cand.at[b, 1], c_s.at[b, 0], c_r.at[b, 0], at(dp, up)),
            remote(cand.at[b, 0], cand.at[b, 2], c_s.at[b, 1], c_r.at[b, 1], at(dp, down)),
        )

    lo, hi = pl.ds(0, half), pl.ds(half, half)

    def c_second(b):
        return (
            remote(cand.at[b, 1, lo], cand.at[b, 3, lo], c_s.at[b, 2], c_r.at[b, 2], at(dp, up)),
            remote(cand.at[b, 2, hi], cand.at[b, 3, hi], c_s.at[b, 3], c_r.at[b, 3], at(dp, down)),
        )

    def offer(b, value):
        cand[b, 0] = value.astype(bf16)
        for copy in c_first(b):
            copy.start()

    def pass_on(b):
        for got, on in zip(c_first(b), c_second(b)):
            got.wait_recv()
            on.start()

    def choose(b):
        for got in c_second(b):
            got.wait_recv()
        away = lax.rem(lax.div(order[b], QUAD) - node + NODES, NODES)
        x = jnp.where(
            away == 0, cand[b, 0],
            jnp.where(away == 3, cand[b, 1], jnp.where(away == 1, cand[b, 2], cand[b, 3])),
        )
        xall[b] = x
        return x

    for k in range(3):
        y_copy(k).wait_recv()
    offer(0, ycur[lax.rem(order[0], QUAD)])

    @pl.loop(0, NB - 1)
    def _(b):
        from_a, from_b, from_core = f_copies(b)
        from_a.wait_recv()
        from_b.wait_recv()
        relay(b).start()
        pass_on(b)
        from_core.wait_recv()
        relay(b).wait_recv()
        following = lax.rem(order[b + 1], QUAD)
        fcrit[...] = jnp.where(
            following == 0, fact[b, 0],
            jnp.where(following == 1, fact[b, 1], jnp.where(following == 2, fact[b, 2], fact[b, 3])),
        )
        x = choose(b)
        offer(b + 1, ycur[following] - lax.dot_general(x, fcrit[...], NT, preferred_element_type=f32))
        for j in range(QUAD):
            ycur[j] = ycur[j] - lax.dot_general(x, fact[b, j], NT, preferred_element_type=f32)

    pass_on(NB - 1)
    choose(NB - 1)

    st[:, :W] = xall[pair[0]]
    st[:, W:] = xall[pair[1]]
    wide = gram.shape[1] // NODES
    tall = parts.shape[0] // ranks
    my_cols = pl.ds(pl.multiple_of(node * wide, wide), wide)
    parts[...] = lax.dot_general(st[...], st[:, my_cols], TN, preferred_element_type=f32).astype(bf16)

    def g_copy(k):
        t = lax.rem(rank + k, ranks)
        return remote(
            parts.at[pl.ds(pl.multiple_of(t * tall, tall), tall)], inbox.at[k - 1],
            g_s.at[k - 1], g_r.at[k - 1], at(lax.div(t, QUAD), base + lax.rem(t, QUAD)),
        )

    @pl.loop(1, ranks)
    def _(k):
        g_copy(k).start()

    for j in range(QUAD):
        place = jnp.int32(0)
        for b in range(NB):
            place = jnp.where(order[b] == base + j, b, place)
        xq[j] = xall[place]
    mine = pl.ds(pl.multiple_of(q * share, share), share)

    def s_copy(k):
        return remote(xq.at[quad[k]], solt.at[mine], s_s.at[k], s_r.at[k], at(dp, base + quad[k]))

    for k in range(3):
        s_copy(k).start()
    solt[mine, :] = xq[q]

    total = parts[pl.ds(pl.multiple_of(rank * tall, tall), tall), :].astype(f32)

    def add(k, total):
        g_copy(k).wait_recv()
        return total + inbox[k - 1].astype(f32)

    total = lax.fori_loop(1, ranks, add, total)
    row = rank * tall + lax.broadcasted_iota(jnp.int32, (tall, wide), 0)
    col = node * wide + lax.broadcasted_iota(jnp.int32, (tall, wide), 1)
    scale = 1.0 / (cols * 8)
    result = jnp.where(row >= col, total * scale, 0.0).astype(bf16)
    piece[...] = result
    my_rows = pl.ds(pl.multiple_of(q * tall, tall), tall)

    def o_copy(k):
        return remote(
            piece, tile.at[my_rows, my_cols], o_s.at[k - 1], o_r.at[k - 1], at(dp, lax.rem(me + k, NB))
        )

    @pl.loop(1, NB)
    def _(k):
        o_copy(k).start()

    tile[my_rows, my_cols] = result

    for k in range(3):
        s_copy(k).wait_recv()
    solved_t[...] = solt[...]

    @pl.loop(0, NB - 1)
    def _(b):
        for copy in f_copies(b):
            copy.wait_send()
        relay(b).wait_send()

    @pl.loop(0, NB)
    def _(b):
        for copy in c_first(b) + c_second(b):
            copy.wait_send()

    for k in range(3):
        y_copy(k).wait_send()
        s_copy(k).wait_send()

    @pl.loop(1, ranks)
    def _(k):
        g_copy(k).wait_send()

    @pl.loop(1, NB)
    def _(k):
        o_copy(k).wait()

    gram[...] = tile[...]


def on_device(factor_rows, diag_inverse, inducing, data_points, lengthscale, carried, block_order, panel_pair):
    cols = data_points.shape[1]
    share = cols // QUAD
    ranks = 8 * QUAD
    side = 2 * W
    smem = pl.BlockSpec(memory_space=pltpu.SMEM)
    vmem = pl.BlockSpec(memory_space=pltpu.VMEM)
    dma = pltpu.SemaphoreType.DMA
    solved_t, gram = pl.pallas_call(
        kernel,
        out_shape=(
            jax.ShapeDtypeStruct((cols, W), bf16),
            jax.ShapeDtypeStruct((side // 8, side), bf16),
        ),
        in_specs=[smem, smem, smem, pl.BlockSpec(memory_space=pl.ANY), vmem, vmem, vmem, vmem],
        out_specs=(vmem, vmem),
        scratch_shapes=[
            pltpu.VMEM((NB - 1, W, W), bf16),
            pltpu.VMEM((NB - 1, QUAD, W, W), bf16),
            pltpu.VMEM((QUAD, share, W), f32),
            pltpu.VMEM((cols, W), f32),
            pltpu.VMEM((NB, NODES, share, W), bf16),
            pltpu.VMEM((NB, share, W), bf16),
            pltpu.VMEM((W, W), bf16),
            pltpu.VMEM((W, W), bf16),
            pltpu.VMEM((QUAD, share, W), bf16),
            pltpu.VMEM((cols, W), bf16),
            pltpu.VMEM((share, side), bf16),
            pltpu.VMEM((side, side // NODES), bf16),
            pltpu.VMEM((ranks - 1, side // ranks, side // NODES), bf16),
            pltpu.VMEM((side // ranks, side // NODES), bf16),
            pltpu.VMEM((side // 8, side), bf16),
            dma((NB - 1,)),
            dma((3,)), dma((3,)),
            dma((NB - 1, 3)), dma((NB - 1, 3)),
            dma((NB - 1,)), dma((NB - 1,)),
            dma((NB, 4)), dma((NB, 4)),
            dma((3,)), dma((3,)),
            dma((ranks - 1,)), dma((ranks - 1,)),
            dma((NB - 1,)), dma((NB - 1,)),
        ],
        compiler_params=pltpu.CompilerParams(
            collective_id=0, has_side_effects=True, vmem_limit_bytes=60 * 1024 * 1024
        ),
        name="substitute",
    )(block_order, panel_pair, lengthscale, factor_rows, diag_inverse, inducing.T, data_points, carried)
    return solved_t.T, gram.astype(f32)


def solution(mesh):
    in_specs = (
        P("ind", None),
        P("ind", None),
        P(None, "ind"),
        P(None, "dp"),
        P(),
        P("ind", "dp"),
        P(),
        P(),
    )
    out_specs = (P("ind", "dp"), P("dp", None))
    return jax.shard_map(
        on_device, mesh=mesh, in_specs=in_specs, out_specs=out_specs, check_vma=False
    )
```

time: 2150 us -> 164 us (0.08)
  waiting for transfers between devices: 1950 us -> 0 us
  Pallas kernels: 0 us -> 158 us
  other arithmetic: 58.1 us -> 1.79 us
  loops' own time: 54.4 us -> 0 us
  local copies, waits for them, and re-layouts: 46.2 us -> 3.34 us
    psum x17 -> x0, waiting for transfers between devices: 1950 us -> none  [the longest x16 1850 us: from_root(): return lax.psum(block, axis)]
    pallas_call x0 -> x1, Pallas kernels: none -> 158 us  [on_device(): pl.pallas_call(kernel, out_shape=(jax.ShapeDtypeStruct((cols, W), bf16),...]
    another operation x33 -> x0, loops' own time: 54.4 us -> none  [the longest x1 54.1 us: on_device(): lax.fori_loop(0, block_count, turn, (residual, solved, first_tile, second...]
    select_n x48 -> x0, other arithmetic: 46.4 us -> none  [the longest x16 17.9 us: record(): second_tile = jnp.where(index == panel_pair[1], panel_now, second_tile)]
    slice x19 -> x0, local copies, waits for them, and re-layouts: 25.9 us -> none  [the longest x16 22.3 us: record(): second_tile = jnp.where(index == panel_pair[1], panel_now, second_tile)]
  transfers between devices with their start and end apart: 17 -> 0, of which waited for: 17 -> 0; matrix products, arithmetic and copies ran while one was open for 1% -> 0% of each run, Pallas kernels for 0% -> 0%
where the time goes in v1:
time: 164 us; the launch traced here: 163 us
  Pallas kernels  158 us (96%)
  local copies, waits for them, and re-layouts  3.34 us (2%)
  other arithmetic  1.79 us (1%)
    pallas_call x1, Pallas kernels, on_device(): pl.pallas_call(kernel, out_shape=(jax.ShapeDtypeStruct((cols, W), bf16),...  158 us
    unnamed x2, local copies, waits for them, and re-layouts  3.34 us

profile of v1, /device:TPU:1, one launch (start us, length us, event | category | flops | bytes accessed | tf_op | source)
XLA Modules:
  0.0 163.3 jit_solution(16312723030775059524)
XLA Ops:
  0.6 1.6 copy.10
  2.2 157.5 %substitute.1 = (bf16[256,512]{1,0:T(8,128)(2,1)}, bf16[128,1024]{1,0:T(8,128)(2,1)}) custom-call(s32[16]{0:T(128)} %order.1, s32[2]{0:T(128)} %pair.1, f32[8]{0:T(128)} %scales.1, bf16[512,8192]{1,0:T(8,128)(2,1)} %factor.1, f32[512,512]{1,0:T(8,128)} %dinv.1, f32[512,8]{1,0:T(8,128)} %bitcast.2, f32[8,256]{1,0:T(8,128)} %points.1, f32[512,256]{1,0:T(8,128)} %carried.1), custom_call_target="tpu_custom_call" | custom-call | tf_op jit(solution)/shard_map/substitute/pallas_call | solution.py:276
  159.7 1.8 %copy.11 = bf16[512,256]{1,0:T(8,128)(2,1)} copy(bf16[512,256]{0,1:T(8,128)(2,1)} %bitcast.3) | data formatting | bytes 524288
  161.5 1.8 %convert_element_type.3 = f32[128,1024]{1,0:T(8,128)} convert(bf16[128,1024]{1,0:T(8,128)(2,1)} %get-tuple-element.5) | non-fusion elementwise | flops 131072 | bytes 786432 | tf_op jit(solution)/shard_map/convert_element_type | solution.py:314

commit v2 on v1

--- a/solution.py
+++ b/solution.py
@@ -18,12 +18,11 @@
 
 def kernel(
     order, pair, scales, factor, dinv, ind_t, points, carried, solved_t, gram,
-    stage, fact, ycur, y0t, cand, xall, fcrit, dbf, xq, solt, st, parts, inbox, piece, tile,
-    n_sem, y_s, y_r, f_s, f_r, l_s, l_r, c_s, c_r, s_s, s_r, g_s, g_r, o_s, o_r,
+    stage, fact, ycur, yin, y0t, cand, xall, fcrit, dbf, xq, solt, st, parts, inbox, piece, tile,
+    n_sem, y_s, y_r, f_s, f_r, l_s, l_r, z_s, z_r, c_s, c_r, s_s, s_r, g_s, g_r, o_s, o_r,
 ):
     cols = points.shape[1]
     share = cols // QUAD
-    half = share // 2
     dp = lax.axis_index("dp")
     me = lax.axis_index("ind")
     node = lax.div(me, QUAD)
@@ -36,7 +35,11 @@
     base = node * QUAD
     up = lax.rem(node + 1, NODES) * QUAD + q
     down = lax.rem(node + NODES - 1, NODES) * QUAD + q
+    across = lax.rem(node + 2, NODES) * QUAD + q
     other_dp = dp + 1 - 2 * lax.rem(dp, 2)
+    z_next = lax.rem(dp + 2, 8)
+    z_last = lax.rem(dp + 6, 8)
+    parity = lax.rem(lax.div(dp, 2), 2)
     rank = dp * QUAD + q
     ranks = 8 * QUAD
 
@@ -80,7 +83,8 @@
         distance = distance + offset * offset
     residual = jnp.exp(-0.5 * distance) - carried[...]
     y0 = jnp.dot(dinv[...], residual, precision=lax.Precision.HIGHEST, preferred_element_type=f32)
-    y0t[...] = y0.T
+    y0 = y0.T
+    y0t[...] = y0.astype(bf16)
     dbf[...] = dinv[...].astype(bf16)
 
     pl.semaphore_wait(barrier, ranks - 1 + NB - QUAD)
@@ -90,25 +94,43 @@
     def y_copy(k):
         to = quad[k]
         return remote(
-            y0t.at[pl.ds(pl.multiple_of(to * share, share), share)], ycur.at[q],
+            y0t.at[pl.ds(pl.multiple_of(to * share, share), share)], yin.at[q],
             y_s.at[k], y_r.at[k], at(dp, base + to),
         )
 
     for k in range(3):
         y_copy(k).start()
-    ycur[q] = y0t[pl.ds(pl.multiple_of(q * share, share), share), :]
-
-    top, bottom = pl.ds(0, W // 2), pl.ds(W // 2, W // 2)
+    ycur[q] = y0t[pl.ds(pl.multiple_of(q * share, share), share), :].astype(f32)
+
+    part = W // 4
+    q_a = pl.ds(pl.multiple_of(2 * parity * part, part), part)
+    q_b = pl.ds(pl.multiple_of((2 * parity + 1) * part, part), part)
 
     def f_copies(b):
         return (
-            remote(fact.at[b, q, top], fact.at[b, q, top], f_s.at[b, 0], f_r.at[b, 0], at(dp, base + q2)),
-            remote(fact.at[b, q, bottom], fact.at[b, q, bottom], f_s.at[b, 1], f_r.at[b, 1], at(other_dp, base + q2)),
+            remote(fact.at[b, q, q_a], fact.at[b, q, q_a], f_s.at[b, 0], f_r.at[b, 0], at(dp, base + q2)),
+            remote(fact.at[b, q, q_b], fact.at[b, q, q_b], f_s.at[b, 1], f_r.at[b, 1], at(other_dp, base + q2)),
             remote(fact.at[b, q], fact.at[b, q], f_s.at[b, 2], f_r.at[b, 2], at(dp, base + q1)),
+        )
+
+    def z_copies(b):
+        return (
+            remote(fact.at[b, q2, q_a], fact.at[b, q2, q_a], z_s.at[b, 0], z_r.at[b, 0], at(z_last, me)),
+            remote(fact.at[b, q2, q_b], fact.at[b, q2, q_b], z_s.at[b, 1], z_r.at[b, 1], at(z_next, me)),
         )
 
     def relay(b):
         return remote(fact.at[b, q2], fact.at[b, q2], l_s.at[b], l_r.at[b], at(dp, base + q1))
+
+    def share_z(b):
+        for got, on in zip(f_copies(b), z_copies(b)):
+            got.wait_recv()
+            on.start()
+
+    def share_core(b):
+        for got in z_copies(b):
+            got.wait_recv()
+        relay(b).start()
 
     @pl.loop(0, NB - 1)
     def _(b):
@@ -117,32 +139,21 @@
         for copy in f_copies(b):
             copy.start()
 
-    def c_first(b):
+    def c_copies(b):
         return (
+            remote(cand.at[b, 0], cand.at[b, 3], c_s.at[b, 2], c_r.at[b, 2], at(dp, across)),
             remote(cand.at[b, 0], cand.at[b, 1], c_s.at[b, 0], c_r.at[b, 0], at(dp, up)),
             remote(cand.at[b, 0], cand.at[b, 2], c_s.at[b, 1], c_r.at[b, 1], at(dp, down)),
         )
 
-    lo, hi = pl.ds(0, half), pl.ds(half, half)
-
-    def c_second(b):
-        return (
-            remote(cand.at[b, 1, lo], cand.at[b, 3, lo], c_s.at[b, 2], c_r.at[b, 2], at(dp, up)),
-            remote(cand.at[b, 2, hi], cand.at[b, 3, hi], c_s.at[b, 3], c_r.at[b, 3], at(dp, down)),
-        )
 
     def offer(b, value):
         cand[b, 0] = value.astype(bf16)
-        for copy in c_first(b):
+        for copy in c_copies(b):
             copy.start()
 
-    def pass_on(b):
-        for got, on in zip(c_first(b), c_second(b)):
-            got.wait_recv()
-            on.start()
-
     def choose(b):
-        for got in c_second(b):
+        for got in c_copies(b):
             got.wait_recv()
         away = lax.rem(lax.div(order[b], QUAD) - node + NODES, NODES)
         x = jnp.where(
@@ -152,18 +163,25 @@
         xall[b] = x
         return x
 
+    share_z(0)
     for k in range(3):
         y_copy(k).wait_recv()
+        ycur[quad[k]] = yin[quad[k]].astype(f32)
     offer(0, ycur[lax.rem(order[0], QUAD)])
+    share_core(0)
+    share_z(1)
 
     @pl.loop(0, NB - 1)
     def _(b):
-        from_a, from_b, from_core = f_copies(b)
-        from_a.wait_recv()
-        from_b.wait_recv()
-        relay(b).start()
-        pass_on(b)
-        from_core.wait_recv()
+        @pl.when(b + 1 < NB - 1)
+        def _():
+            share_core(b + 1)
+
+        @pl.when(b + 2 < NB - 1)
+        def _():
+            share_z(b + 2)
+
+        f_copies(b)[2].wait_recv()
         relay(b).wait_recv()
         following = lax.rem(order[b + 1], QUAD)
         fcrit[...] = jnp.where(
@@ -175,7 +193,6 @@
         for j in range(QUAD):
             ycur[j] = ycur[j] - lax.dot_general(x, fact[b, j], NT, preferred_element_type=f32)
 
-    pass_on(NB - 1)
     choose(NB - 1)
 
     st[:, :W] = xall[pair[0]]
@@ -241,13 +258,13 @@
 
     @pl.loop(0, NB - 1)
     def _(b):
-        for copy in f_copies(b):
+        for copy in f_copies(b) + z_copies(b):
             copy.wait_send()
         relay(b).wait_send()
 
     @pl.loop(0, NB)
     def _(b):
-        for copy in c_first(b) + c_second(b):
+        for copy in c_copies(b):
             copy.wait_send()
 
     for k in range(3):
@@ -285,7 +302,8 @@
             pltpu.VMEM((NB - 1, W, W), bf16),
             pltpu.VMEM((NB - 1, QUAD, W, W), bf16),
             pltpu.VMEM((QUAD, share, W), f32),
-            pltpu.VMEM((cols, W), f32),
+            pltpu.VMEM((QUAD, share, W), bf16),
+            pltpu.VMEM((cols, W), bf16),
             pltpu.VMEM((NB, NODES, share, W), bf16),
             pltpu.VMEM((NB, share, W), bf16),
             pltpu.VMEM((W, W), bf16),
@@ -301,7 +319,8 @@
             dma((3,)), dma((3,)),
             dma((NB - 1, 3)), dma((NB - 1, 3)),
             dma((NB - 1,)), dma((NB - 1,)),
-            dma((NB, 4)), dma((NB, 4)),
+            dma((NB - 1, 2)), dma((NB - 1, 2)),
+            dma((NB, 3)), dma((NB, 3)),
             dma((3,)), dma((3,)),
             dma((ranks - 1,)), dma((ranks - 1,)),
             dma((NB - 1,)), dma((NB - 1,)),

time: 164 us -> 127 us (0.77)
  Pallas kernels: 158 us -> 121 us
    pallas_call x1, Pallas kernels: 158 us -> 121 us  [on_device(): pl.pallas_call(kernel, out_shape=(jax.ShapeDtypeStruct((cols, W), bf16),...]
where the time goes in v2:
time: 127 us
  Pallas kernels  121 us (95%)
  local copies, waits for them, and re-layouts  3.34 us (3%)
  other arithmetic  1.79 us (1%)
    pallas_call x1, Pallas kernels, on_device(): pl.pallas_call(kernel, out_shape=(jax.ShapeDtypeStruct((cols, W), bf16),...  121 us
    unnamed x2, local copies, waits for them, and re-layouts  3.34 us

profile of v2, /device:TPU:1, one launch (start us, length us, event | category | flops | bytes accessed | tf_op | source)
XLA Modules:
  0.0 126.8 jit_solution(4518701436534029483)
XLA Ops:
  0.6 1.6 %copy.10 = f32[8,512]{0,1:T(8,128)} copy(f32[8,512]{1,0:T(8,128)} %param.10) | data formatting | bytes 32768 | tf_op args[2]
  2.2 121.1 %substitute.1 = (bf16[256,512]{1,0:T(8,128)(2,1)}, bf16[128,1024]{1,0:T(8,128)(2,1)}) custom-call(s32[16]{0:T(128)} %order.1, s32[2]{0:T(128)} %pair.1, f32[8]{0:T(128)} %scales.1, bf16[512,8192]{1,0:T(8,128)(2,1)} %factor.1, f32[512,512]{1,0:T(8,128)} %dinv.1, f32[512,8]{1,0:T(8,128)} %bitcast.2, f32[8,256]{1,0:T(8,128)} %points.1, f32[512,256]{1,0:T(8,128)} %carried.1), custom_call_target="tpu_custom_call" | custom-call | tf_op jit(solution)/shard_map/substitute/pallas_call | solution.py:293
  123.3 1.8 %copy.11 = bf16[512,256]{1,0:T(8,128)(2,1)} copy(bf16[512,256]{0,1:T(8,128)(2,1)} %bitcast.3) | data formatting | bytes 524288
  125.0 1.8 %convert_element_type.3 = f32[128,1024]{1,0:T(8,128)} convert(bf16[128,1024]{1,0:T(8,128)(2,1)} %get-tuple-element.5) | non-fusion elementwise | flops 131072 | bytes 786432 | tf_op jit(solution)/shard_map/convert_element_type | solution.py:333

commit v3 on v2

--- a/solution.py
+++ b/solution.py
@@ -14,10 +14,11 @@
 bf16 = jnp.bfloat16
 
 NB, W, NODES, QUAD = 16, 512, 4, 4
+LEAD, ZLEAD, HALVES = 6, 3, 4
 
 
 def kernel(
-    order, pair, scales, factor, dinv, ind_t, points, carried, solved_t, gram,
+    order, pair, scales, factor, dinv, inducing, points, carried, solved_t, gram,
     stage, fact, ycur, yin, y0t, cand, xall, fcrit, dbf, xq, solt, st, parts, inbox, piece, tile,
     n_sem, y_s, y_r, f_s, f_r, l_s, l_r, z_s, z_r, c_s, c_r, s_s, s_r, g_s, g_r, o_s, o_r,
 ):
@@ -76,10 +77,11 @@
             barrier, inc=1, device_id=at(dp, lax.rem(base + QUAD + k, NB)), device_id_type=MESH
         )
 
+    along = inducing[...].T
     distance = jnp.zeros((W, cols), f32)
     for feature in range(points.shape[0]):
         inverse = jnp.full((1, 1), 1.0, f32) / scales[feature]
-        offset = (ind_t[:, feature : feature + 1] - points[feature : feature + 1, :]) * inverse
+        offset = (along[:, feature : feature + 1] - points[feature : feature + 1, :]) * inverse
         distance = distance + offset * offset
     residual = jnp.exp(-0.5 * distance) - carried[...]
     y0 = jnp.dot(dinv[...], residual, precision=lax.Precision.HIGHEST, preferred_element_type=f32)
@@ -132,54 +134,66 @@
             got.wait_recv()
         relay(b).start()
 
-    @pl.loop(0, NB - 1)
-    def _(b):
+    def make(b):
         n_copy(b).wait()
         fact[b, q] = jnp.dot(dbf[...], stage[b], preferred_element_type=f32).astype(bf16)
         for copy in f_copies(b):
             copy.start()
 
-    def c_copies(b):
-        return (
-            remote(cand.at[b, 0], cand.at[b, 3], c_s.at[b, 2], c_r.at[b, 2], at(dp, across)),
-            remote(cand.at[b, 0], cand.at[b, 1], c_s.at[b, 0], c_r.at[b, 0], at(dp, up)),
-            remote(cand.at[b, 0], cand.at[b, 2], c_s.at[b, 1], c_r.at[b, 1], at(dp, down)),
-        )
-
-
-    def offer(b, value):
-        cand[b, 0] = value.astype(bf16)
-        for copy in c_copies(b):
+    half = share // HALVES
+
+    def c_copies(b, h):
+        rows = pl.ds(h * half, half)
+        return tuple(
+            remote(cand.at[b, 0, rows], cand.at[b, n + 1, rows], c_s.at[b, h, n], c_r.at[b, h, n], at(dp, to))
+            for n, to in ((2, across), (0, up), (1, down))
+        )
+
+    def offer(b, h, value):
+        cand[b, 0, pl.ds(h * half, half)] = value.astype(bf16)
+        for copy in c_copies(b, h):
             copy.start()
 
-    def choose(b):
-        for got in c_copies(b):
+    def choose(b, h):
+        rows = pl.ds(h * half, half)
+        for got in c_copies(b, h):
             got.wait_recv()
         away = lax.rem(lax.div(order[b], QUAD) - node + NODES, NODES)
         x = jnp.where(
-            away == 0, cand[b, 0],
-            jnp.where(away == 3, cand[b, 1], jnp.where(away == 1, cand[b, 2], cand[b, 3])),
-        )
-        xall[b] = x
+            away == 0, cand[b, 0, rows],
+            jnp.where(away == 3, cand[b, 1, rows], jnp.where(away == 1, cand[b, 2, rows], cand[b, 3, rows])),
+        )
+        xall[b, rows] = x
         return x
+
+    @pl.loop(0, LEAD)
+    def _(b):
+        make(b)
 
     share_z(0)
     for k in range(3):
         y_copy(k).wait_recv()
         ycur[quad[k]] = yin[quad[k]].astype(f32)
-    offer(0, ycur[lax.rem(order[0], QUAD)])
+    first = lax.rem(order[0], QUAD)
+    for h in range(HALVES):
+        offer(0, h, ycur[first, pl.ds(h * half, half)])
+    for b in range(1, ZLEAD):
+        share_z(b)
     share_core(0)
-    share_z(1)
 
     @pl.loop(0, NB - 1)
     def _(b):
+        @pl.when(b + LEAD < NB - 1)
+        def _():
+            make(b + LEAD)
+
+        @pl.when(b + ZLEAD < NB - 1)
+        def _():
+            share_z(b + ZLEAD)
+
         @pl.when(b + 1 < NB - 1)
         def _():
             share_core(b + 1)
-
-        @pl.when(b + 2 < NB - 1)
-        def _():
-            share_z(b + 2)
 
         f_copies(b)[2].wait_recv()
         relay(b).wait_recv()
@@ -188,12 +202,15 @@
             following == 0, fact[b, 0],
             jnp.where(following == 1, fact[b, 1], jnp.where(following == 2, fact[b, 2], fact[b, 3])),
         )
-        x = choose(b)
-        offer(b + 1, ycur[following] - lax.dot_general(x, fcrit[...], NT, preferred_element_type=f32))
+        for h in range(HALVES):
+            x = choose(b, h)
+            known = ycur[following, pl.ds(h * half, half)]
+            offer(b + 1, h, known - lax.dot_general(x, fcrit[...], NT, preferred_element_type=f32))
         for j in range(QUAD):
-            ycur[j] = ycur[j] - lax.dot_general(x, fact[b, j], NT, preferred_element_type=f32)
-
-    choose(NB - 1)
+            ycur[j] = ycur[j] - lax.dot_general(xall[b], fact[b, j], NT, preferred_element_type=f32)
+
+    for h in range(HALVES):
+        choose(NB - 1, h)
 
     st[:, :W] = xall[pair[0]]
     st[:, W:] = xall[pair[1]]
@@ -264,8 +281,9 @@
 
     @pl.loop(0, NB)
     def _(b):
-        for copy in c_copies(b):
-            copy.wait_send()
+        for h in range(HALVES):
+            for copy in c_copies(b, h):
+                copy.wait_send()
 
     for k in range(3):
         y_copy(k).wait_send()
@@ -320,7 +338,7 @@
             dma((NB - 1, 3)), dma((NB - 1, 3)),
             dma((NB - 1,)), dma((NB - 1,)),
             dma((NB - 1, 2)), dma((NB - 1, 2)),
-            dma((NB, 3)), dma((NB, 3)),
+            dma((NB, HALVES, 3)), dma((NB, HALVES, 3)),
             dma((3,)), dma((3,)),
             dma((ranks - 1,)), dma((ranks - 1,)),
             dma((NB - 1,)), dma((NB - 1,)),
@@ -329,7 +347,7 @@
             collective_id=0, has_side_effects=True, vmem_limit_bytes=60 * 1024 * 1024
         ),
         name="substitute",
-    )(block_order, panel_pair, lengthscale, factor_rows, diag_inverse, inducing.T, data_points, carried)
+    )(block_order, panel_pair, lengthscale, factor_rows, diag_inverse, inducing, data_points, carried)
     return solved_t.T, gram.astype(f32)
 
 

time: 127 us -> 112 us (0.88)
  Pallas kernels: 121 us -> 108 us
  local copies, waits for them, and re-layouts: 3.34 us -> 1.79 us
    pallas_call x1, Pallas kernels: 121 us -> 108 us  [on_device(): pl.pallas_call(kernel, out_shape=(jax.ShapeDtypeStruct((cols, W), bf16),...]
    unnamed x2 -> x1, local copies, waits for them, and re-layouts: 3.34 us -> 1.79 us
where the time goes in v3:
time: 112 us
  Pallas kernels  108 us (96%)
  local copies, waits for them, and re-layouts  1.79 us (2%)
  other arithmetic  1.79 us (2%)
    pallas_call x1, Pallas kernels, on_device(): pl.pallas_call(kernel, out_shape=(jax.ShapeDtypeStruct((cols, W), bf16),...  108 us

profile of v3, /device:TPU:1, one launch (start us, length us, event | category | flops | bytes accessed | tf_op | source)
XLA Modules:
  0.0 112.2 jit_solution(13677877781344105112)
XLA Ops:
  0.6 108.0 %substitute.1 = (bf16[256,512]{1,0:T(8,128)(2,1)}, bf16[128,1024]{1,0:T(8,128)(2,1)}) custom-call(s32[16]{0:T(128)} %order.1, s32[2]{0:T(128)} %pair.1, f32[8]{0:T(128)} %scales.1, bf16[512,8192]{1,0:T(8,128)(2,1)} %factor.1, f32[512,512]{1,0:T(8,128)} %dinv.1, f32[8,512]{1,0:T(8,128)} %inducing.1, f32[8,256]{1,0:T(8,128)} %points.1, f32[512,256]{1,0:T(8,128)} %carried.1), custom_call_target="tpu_custom_call" | custom-call | tf_op jit(solution)/shard_map/substitute/pallas_call | solution.py:311
  108.6 1.8 %copy.10 = bf16[512,256]{1,0:T(8,128)(2,1)} copy(bf16[512,256]{0,1:T(8,128)(2,1)} %bitcast.1) | data formatting | bytes 524288
  110.4 1.8 %convert_element_type.3 = f32[128,1024]{1,0:T(8,128)} convert(bf16[128,1024]{1,0:T(8,128)(2,1)} %get-tuple-element.5) | non-fusion elementwise | flops 131072 | bytes 786432 | tf_op jit(solution)/shard_map/convert_element_type | solution.py:351

commit v4 on v3

--- a/solution.py
+++ b/solution.py
@@ -14,13 +14,13 @@
 bf16 = jnp.bfloat16
 
 NB, W, NODES, QUAD = 16, 512, 4, 4
-LEAD, ZLEAD, HALVES = 6, 3, 4
+SOON, LEAD, HALVES = 3, 6, 4
 
 
 def kernel(
-    order, pair, scales, factor, dinv, inducing, points, carried, solved_t, gram,
-    stage, fact, ycur, yin, y0t, cand, xall, fcrit, dbf, xq, solt, st, parts, inbox, piece, tile,
-    n_sem, y_s, y_r, f_s, f_r, l_s, l_r, z_s, z_r, c_s, c_r, s_s, s_r, g_s, g_r, o_s, o_r,
+    order, pair, scales, factor, inverse_hbm, carried_hbm, inducing, points, solved_t, gram,
+    dinv, carried, stage, fact, ycur, yin, y0t, cand, xall, fcrit, dbf, xq, solt, st, parts, inbox, piece, tile,
+    i_sem, n_sem, y_s, y_r, f_s, f_r, l_s, l_r, z_s, z_r, c_s, c_r, s_s, s_r, g_s, g_r, o_s, o_r,
 ):
     cols = points.shape[1]
     share = cols // QUAD
@@ -58,24 +58,31 @@
             factor.at[:, pl.ds(pl.multiple_of(b * W, W), W)], stage.at[b], n_sem.at[b]
         )
 
-    @pl.loop(0, NB - 1)
+    d_copy = pltpu.make_async_copy(inverse_hbm, dinv, i_sem.at[0])
+    r_copy = pltpu.make_async_copy(carried_hbm, carried, i_sem.at[1])
+    d_copy.start()
+    n_copy(0).start()
+    r_copy.start()
+
+    @pl.loop(1, NB - 1)
     def _(b):
         n_copy(b).start()
 
     barrier = pltpu.get_barrier_semaphore()
-
-    @pl.loop(1, ranks)
-    def _(k):
-        t = lax.rem(rank + k, ranks)
-        pl.semaphore_signal(
-            barrier, inc=1, device_id=at(lax.div(t, QUAD), base + lax.rem(t, QUAD)), device_id_type=MESH
-        )
-
-    @pl.loop(0, NB - QUAD)
-    def _(k):
-        pl.semaphore_signal(
-            barrier, inc=1, device_id=at(dp, lax.rem(base + QUAD + k, NB)), device_id_type=MESH
-        )
+    near = (
+        at(dp, up), at(dp, down), at(dp, across), at(dp, base + q2), at(other_dp, base + q2),
+        at(z_next, me), at(z_last, me), at(dp, base + q3), at(dp, base + q1),
+    )
+    for device in near:
+        pl.semaphore_signal(barrier, inc=1, device_id=device, device_id_type=MESH)
+
+    def compute(b):
+        n_copy(b).wait()
+        fact[b, q] = jnp.dot(dbf[...], stage[b], preferred_element_type=f32).astype(bf16)
+
+    d_copy.wait()
+    dbf[...] = dinv[...].astype(bf16)
+    compute(0)
 
     along = inducing[...].T
     distance = jnp.zeros((W, cols), f32)
@@ -83,13 +90,13 @@
         inverse = jnp.full((1, 1), 1.0, f32) / scales[feature]
         offset = (along[:, feature : feature + 1] - points[feature : feature + 1, :]) * inverse
         distance = distance + offset * offset
+    r_copy.wait()
     residual = jnp.exp(-0.5 * distance) - carried[...]
     y0 = jnp.dot(dinv[...], residual, precision=lax.Precision.HIGHEST, preferred_element_type=f32)
     y0 = y0.T
     y0t[...] = y0.astype(bf16)
-    dbf[...] = dinv[...].astype(bf16)
-
-    pl.semaphore_wait(barrier, ranks - 1 + NB - QUAD)
+
+    pl.semaphore_wait(barrier, len(near))
 
     quad = (q2, q3, q1)
 
@@ -100,9 +107,6 @@
             y_s.at[k], y_r.at[k], at(dp, base + to),
         )
 
-    for k in range(3):
-        y_copy(k).start()
-    ycur[q] = y0t[pl.ds(pl.multiple_of(q * share, share), share), :].astype(f32)
 
     part = W // 4
     q_a = pl.ds(pl.multiple_of(2 * parity * part, part), part)
@@ -134,11 +138,13 @@
             got.wait_recv()
         relay(b).start()
 
-    def make(b):
-        n_copy(b).wait()
-        fact[b, q] = jnp.dot(dbf[...], stage[b], preferred_element_type=f32).astype(bf16)
+    def send(b):
         for copy in f_copies(b):
             copy.start()
+
+    def make(b):
+        compute(b)
+        send(b)
 
     half = share // HALVES
 
@@ -166,7 +172,12 @@
         xall[b, rows] = x
         return x
 
-    @pl.loop(0, LEAD)
+    send(0)
+    for k in range(3):
+        y_copy(k).start()
+    ycur[q] = y0t[pl.ds(pl.multiple_of(q * share, share), share), :].astype(f32)
+
+    @pl.loop(1, SOON)
     def _(b):
         make(b)
 
@@ -177,21 +188,32 @@
     first = lax.rem(order[0], QUAD)
     for h in range(HALVES):
         offer(0, h, ycur[first, pl.ds(h * half, half)])
-    for b in range(1, ZLEAD):
-        share_z(b)
+
+    @pl.loop(SOON, LEAD)
+    def _(b):
+        make(b)
+
     share_core(0)
+    share_z(1)
+    early = {
+        1: ((share_z, 2), (share_core, 1)),
+        2: ((share_z, 3), (share_core, 2), (share_z, 4)),
+        3: ((share_core, 3), (share_z, 5), (share_core, 4), (share_z, 6)),
+    }
 
     @pl.loop(0, NB - 1)
     def _(b):
-        @pl.when(b + LEAD < NB - 1)
+        for step, work in early.items():
+            @pl.when(b == step)
+            def _():
+                for share, block in work:
+                    share(block)
+
+        @pl.when((b > max(early)) & (b + 3 < NB - 1))
         def _():
-            make(b + LEAD)
-
-        @pl.when(b + ZLEAD < NB - 1)
-        def _():
-            share_z(b + ZLEAD)
-
-        @pl.when(b + 1 < NB - 1)
+            share_z(b + 3)
+
+        @pl.when((b > max(early)) & (b + 1 < NB - 1))
         def _():
             share_core(b + 1)
 
@@ -208,6 +230,10 @@
             offer(b + 1, h, known - lax.dot_general(x, fcrit[...], NT, preferred_element_type=f32))
         for j in range(QUAD):
             ycur[j] = ycur[j] - lax.dot_general(xall[b], fact[b, j], NT, preferred_element_type=f32)
+
+        @pl.when(b + LEAD < NB - 1)
+        def _():
+            make(b + LEAD)
 
     for h in range(HALVES):
         choose(NB - 1, h)
@@ -300,6 +326,19 @@
     gram[...] = tile[...]
 
 
+def finish(solved_t, gram):
+    def body(solved_t, gram, solved, gram_out):
+        solved[...] = solved_t[...].T
+        gram_out[...] = gram[...].astype(f32)
+
+    cols, rows = solved_t.shape
+    return pl.pallas_call(
+        body,
+        out_shape=(jax.ShapeDtypeStruct((rows, cols), bf16), jax.ShapeDtypeStruct(gram.shape, f32)),
+        name="finish",
+    )(solved_t, gram)
+
+
 def on_device(factor_rows, diag_inverse, inducing, data_points, lengthscale, carried, block_order, panel_pair):
     cols = data_points.shape[1]
     share = cols // QUAD
@@ -307,6 +346,7 @@
     side = 2 * W
     smem = pl.BlockSpec(memory_space=pltpu.SMEM)
     vmem = pl.BlockSpec(memory_space=pltpu.VMEM)
+    hbm = pl.BlockSpec(memory_space=pl.ANY)
     dma = pltpu.SemaphoreType.DMA
     solved_t, gram = pl.pallas_call(
         kernel,
@@ -314,9 +354,11 @@
             jax.ShapeDtypeStruct((cols, W), bf16),
             jax.ShapeDtypeStruct((side // 8, side), bf16),
         ),
-        in_specs=[smem, smem, smem, pl.BlockSpec(memory_space=pl.ANY), vmem, vmem, vmem, vmem],
+        in_specs=[smem, smem, smem, hbm, hbm, hbm, vmem, vmem],
         out_specs=(vmem, vmem),
         scratch_shapes=[
+            pltpu.VMEM((W, W), f32),
+            pltpu.VMEM((W, cols), f32),
             pltpu.VMEM((NB - 1, W, W), bf16),
             pltpu.VMEM((NB - 1, QUAD, W, W), bf16),
             pltpu.VMEM((QUAD, share, W), f32),
@@ -333,6 +375,7 @@
             pltpu.VMEM((ranks - 1, side // ranks, side // NODES), bf16),
             pltpu.VMEM((side // ranks, side // NODES), bf16),
             pltpu.VMEM((side // 8, side), bf16),
+            dma((2,)),
             dma((NB - 1,)),
             dma((3,)), dma((3,)),
             dma((NB - 1, 3)), dma((NB - 1, 3)),
@@ -347,8 +390,8 @@
             collective_id=0, has_side_effects=True, vmem_limit_bytes=60 * 1024 * 1024
         ),
         name="substitute",
-    )(block_order, panel_pair, lengthscale, factor_rows, diag_inverse, inducing, data_points, carried)
-    return solved_t.T, gram.astype(f32)
+    )(block_order, panel_pair, lengthscale, factor_rows, diag_inverse, carried, inducing, data_points)
+    return finish(solved_t, gram)
 
 
 def solution(mesh):

time: 112 us -> 109 us (0.973)
  other arithmetic: 1.79 us -> 0 us
  local copies, waits for them, and re-layouts: 1.79 us -> 0 us
    pallas_call x1, Pallas kernels: 108 us -> 106 us  [on_device(): pl.pallas_call(kernel, out_shape=(jax.ShapeDtypeStruct((cols, W), bf16),...]
    pallas_call x0 -> x1, Pallas kernels: none -> 1.97 us  [finish(): pl.pallas_call(body, out_shape=(jax.ShapeDtypeStruct((rows, cols), bf16),...]
    convert_element_type x1 -> x0, other arithmetic: 1.79 us -> none  [on_device(): return (solved_t.T, gram.astype(f32))]
    unnamed x1 -> x0, local copies, waits for them, and re-layouts: 1.79 us -> none
where the time goes in v4:
time: 109 us
  Pallas kernels  108 us (99%)
    pallas_call x1, Pallas kernels, on_device(): pl.pallas_call(kernel, out_shape=(jax.ShapeDtypeStruct((cols, W), bf16),...  106 us

profile of v4, /device:TPU:1, one launch (start us, length us, event | category | flops | bytes accessed | tf_op | source)
XLA Modules:
  0.0 108.5 jit_solution(17779216839249558048)
XLA Ops:
  0.6 105.9 %substitute.1 = (bf16[256,512]{1,0:T(8,128)(2,1)}, bf16[128,1024]{1,0:T(8,128)(2,1)}) custom-call(s32[16]{0:T(128)} %order.1, s32[2]{0:T(128)} %pair.1, f32[8]{0:T(128)} %scales.1, bf16[512,8192]{1,0:T(8,128)(2,1)} %factor.1, f32[512,512]{1,0:T(8,128)} %inverse_hbm.1, f32[512,256]{1,0:T(8,128)} %carried_hbm.1, f32[8,512]{1,0:T(8,128)} %inducing.1, ...), custom_call_target="tpu_custom_call" | custom-call | tf_op jit(solution)/shard_map/substitute/pallas_call | solution.py:351
  106.6 2.0 %finish.1 = (bf16[512,256]{1,0:T(8,128)(2,1)}, f32[128,1024]{1,0:T(8,128)}) custom-call(bf16[256,512]{1,0:T(8,128)(2,1)} %get-tuple-element.4.solved_t, bf16[128,1024]{1,0:T(8,128)(2,1)} %get-tuple-element.5.gram), custom_call_target="tpu_custom_call" | custom-call | tf_op jit(solution)/shard_map/finish/pallas_call | solution.py:335

commit v5 on v4

--- a/solution.py
+++ b/solution.py
@@ -8,13 +8,13 @@
 from jax.sharding import PartitionSpec as P
 
 MESH = pl.DeviceIdType.MESH
-NT = (((1,), (1,)), ((), ()))
+TT = (((0,), (1,)), ((), ()))
 TN = (((0,), (0,)), ((), ()))
 f32 = jnp.float32
 bf16 = jnp.bfloat16
 
 NB, W, NODES, QUAD = 16, 512, 4, 4
-SOON, LEAD, HALVES = 3, 6, 4
+SOON, LEAD, HALVES, FIRST = 3, 6, 4, 0
 
 
 def kernel(
@@ -78,7 +78,7 @@
 
     def compute(b):
         n_copy(b).wait()
-        fact[b, q] = jnp.dot(dbf[...], stage[b], preferred_element_type=f32).astype(bf16)
+        fact[b, q] = lax.dot_general(stage[b], dbf[...], TT, preferred_element_type=f32).astype(bf16)
 
     d_copy.wait()
     dbf[...] = dinv[...].astype(bf16)
@@ -100,11 +100,13 @@
 
     quad = (q2, q3, q1)
 
-    def y_copy(k):
+    half = share // HALVES
+
+    def y_copy(k, h):
         to = quad[k]
         return remote(
-            y0t.at[pl.ds(pl.multiple_of(to * share, share), share)], yin.at[q],
-            y_s.at[k], y_r.at[k], at(dp, base + to),
+            y0t.at[pl.ds(pl.multiple_of(to * share + h * half, half), half)], yin.at[q, pl.ds(h * half, half)],
+            y_s.at[h, k], y_r.at[h, k], at(dp, base + to),
         )
 
 
@@ -125,18 +127,25 @@
             remote(fact.at[b, q2, q_b], fact.at[b, q2, q_b], z_s.at[b, 1], z_r.at[b, 1], at(z_next, me)),
         )
 
-    def relay(b):
-        return remote(fact.at[b, q2], fact.at[b, q2], l_s.at[b], l_r.at[b], at(dp, base + q1))
+    mine_x = pl.ds(pl.multiple_of(2 * parity * part, part), 2 * part)
+    mine_z = pl.ds(pl.multiple_of(2 * (1 - parity) * part, part), 2 * part)
+
+    def relays(b):
+        return tuple(
+            remote(fact.at[b, q2, rows], fact.at[b, q2, rows], l_s.at[b, n], l_r.at[b, n], at(dp, base + q1))
+            for n, rows in enumerate((mine_x, mine_z))
+        )
 
     def share_z(b):
         for got, on in zip(f_copies(b), z_copies(b)):
             got.wait_recv()
             on.start()
+        relays(b)[0].start()
 
     def share_core(b):
         for got in z_copies(b):
             got.wait_recv()
-        relay(b).start()
+        relays(b)[1].start()
 
     def send(b):
         for copy in f_copies(b):
@@ -146,7 +155,6 @@
         compute(b)
         send(b)
 
-    half = share // HALVES
 
     def c_copies(b, h):
         rows = pl.ds(h * half, half)
@@ -172,22 +180,34 @@
         xall[b, rows] = x
         return x
 
-    send(0)
-    for k in range(3):
-        y_copy(k).start()
+    for h in range(HALVES):
+        if h == FIRST:
+            send(0)
+        for k in range(3):
+            y_copy(k, h).start()
     ycur[q] = y0t[pl.ds(pl.multiple_of(q * share, share), share), :].astype(f32)
+
+    def f_sent(b):
+        for copy in f_copies(b) + z_copies(b) + relays(b):
+            copy.wait_send()
+
+    def c_sent(b):
+        for h in range(HALVES):
+            for copy in c_copies(b, h):
+                copy.wait_send()
 
     @pl.loop(1, SOON)
     def _(b):
         make(b)
 
     share_z(0)
-    for k in range(3):
-        y_copy(k).wait_recv()
-        ycur[quad[k]] = yin[quad[k]].astype(f32)
     first = lax.rem(order[0], QUAD)
     for h in range(HALVES):
-        offer(0, h, ycur[first, pl.ds(h * half, half)])
+        rows = pl.ds(h * half, half)
+        for k in range(3):
+            y_copy(k, h).wait_recv()
+            ycur[quad[k], rows] = yin[quad[k], rows].astype(f32)
+        offer(0, h, ycur[first, rows])
 
     @pl.loop(SOON, LEAD)
     def _(b):
@@ -218,7 +238,8 @@
             share_core(b + 1)
 
         f_copies(b)[2].wait_recv()
-        relay(b).wait_recv()
+        for got in relays(b):
+            got.wait_recv()
         following = lax.rem(order[b + 1], QUAD)
         fcrit[...] = jnp.where(
             following == 0, fact[b, 0],
@@ -227,13 +248,19 @@
         for h in range(HALVES):
             x = choose(b, h)
             known = ycur[following, pl.ds(h * half, half)]
-            offer(b + 1, h, known - lax.dot_general(x, fcrit[...], NT, preferred_element_type=f32))
+            offer(b + 1, h, known - jnp.dot(x, fcrit[...], preferred_element_type=f32))
         for j in range(QUAD):
-            ycur[j] = ycur[j] - lax.dot_general(xall[b], fact[b, j], NT, preferred_element_type=f32)
+            ycur[j] = ycur[j] - jnp.dot(xall[b], fact[b, j], preferred_element_type=f32)
 
         @pl.when(b + LEAD < NB - 1)
         def _():
             make(b + LEAD)
+
+        c_sent(b)
+
+        @pl.when(b > 0)
+        def _():
+            f_sent(b - 1)
 
     for h in range(HALVES):
         choose(NB - 1, h)
@@ -299,20 +326,12 @@
         s_copy(k).wait_recv()
     solved_t[...] = solt[...]
 
-    @pl.loop(0, NB - 1)
-    def _(b):
-        for copy in f_copies(b) + z_copies(b):
-            copy.wait_send()
-        relay(b).wait_send()
-
-    @pl.loop(0, NB)
-    def _(b):
+    f_sent(NB - 2)
+    c_sent(NB - 1)
+
+    for k in range(3):
         for h in range(HALVES):
-            for copy in c_copies(b, h):
-                copy.wait_send()
-
-    for k in range(3):
-        y_copy(k).wait_send()
+            y_copy(k, h).wait_send()
         s_copy(k).wait_send()
 
     @pl.loop(1, ranks)
@@ -377,9 +396,9 @@
             pltpu.VMEM((side // 8, side), bf16),
             dma((2,)),
             dma((NB - 1,)),
-            dma((3,)), dma((3,)),
+            dma((HALVES, 3)), dma((HALVES, 3)),
             dma((NB - 1, 3)), dma((NB - 1, 3)),
-            dma((NB - 1,)), dma((NB - 1,)),
+            dma((NB - 1, 2)), dma((NB - 1, 2)),
             dma((NB - 1, 2)), dma((NB - 1, 2)),
             dma((NB, HALVES, 3)), dma((NB, HALVES, 3)),
             dma((3,)), dma((3,)),

time: 109 us -> 107 us (0.982)
    pallas_call x1, Pallas kernels: 106 us -> 105 us  [on_device(): pl.pallas_call(kernel, out_shape=(jax.ShapeDtypeStruct((cols, W), bf16),...]
where the time goes in v5:
time: 107 us
  Pallas kernels  107 us (100%)
    pallas_call x1, Pallas kernels, on_device(): pl.pallas_call(kernel, out_shape=(jax.ShapeDtypeStruct((cols, W), bf16),...  105 us

profile of v5, /device:TPU:1, one launch (start us, length us, event | category | flops | bytes accessed | tf_op | source)
XLA Modules:
  0.0 107.2 jit_solution(16987080311214398980)
XLA Ops:
  0.6 104.6 %substitute.1 = (bf16[256,512]{1,0:T(8,128)(2,1)}, bf16[128,1024]{1,0:T(8,128)(2,1)}) custom-call(s32[16]{0:T(128)} %order.1, s32[2]{0:T(128)} %pair.1, f32[8]{0:T(128)} %scales.1, bf16[512,8192]{1,0:T(8,128)(2,1)} %factor.1, f32[512,512]{1,0:T(8,128)} %inverse_hbm.1, f32[512,256]{1,0:T(8,128)} %carried_hbm.1, f32[8,512]{1,0:T(8,128)} %inducing.1, ...), custom_call_target="tpu_custom_call" | custom-call | tf_op jit(solution)/shard_map/substitute/pallas_call | solution.py:370
  105.2 2.0 %finish.1 = (bf16[512,256]{1,0:T(8,128)(2,1)}, f32[128,1024]{1,0:T(8,128)}) custom-call(bf16[256,512]{1,0:T(8,128)(2,1)} %get-tuple-element.4.solved_t, bf16[128,1024]{1,0:T(8,128)(2,1)} %get-tuple-element.5.gram), custom_call_target="tpu_custom_call" | custom-call | tf_op jit(solution)/shard_map/finish/pallas_call | solution.py:354

commit v6 on v5

--- a/solution.py
+++ b/solution.py
@@ -14,7 +14,7 @@
 bf16 = jnp.bfloat16
 
 NB, W, NODES, QUAD = 16, 512, 4, 4
-SOON, LEAD, HALVES, FIRST = 3, 6, 4, 0
+SOON, LEAD, HALVES, FIRST = 4, 7, 4, 0
 
 
 def kernel(

time: 107 us -> 107 us (level)
  no operation moved by 1% of the time
where the time goes in v6:
time: 107 us
  Pallas kernels  106 us (99%)
    pallas_call x1, Pallas kernels, on_device(): pl.pallas_call(kernel, out_shape=(jax.ShapeDtypeStruct((cols, W), bf16),...  104 us

profile of v6, /device:TPU:1, one launch (start us, length us, event | category | flops | bytes accessed | tf_op | source)
XLA Modules:
  0.0 107.1 jit_solution(12712216568485625189)
XLA Ops:
  0.6 104.5 %substitute.1 = (bf16[256,512]{1,0:T(8,128)(2,1)}, bf16[128,1024]{1,0:T(8,128)(2,1)}) custom-call(s32[16]{0:T(128)} %order.1, s32[2]{0:T(128)} %pair.1, f32[8]{0:T(128)} %scales.1, bf16[512,8192]{1,0:T(8,128)(2,1)} %factor.1, f32[512,512]{1,0:T(8,128)} %inverse_hbm.1, f32[512,256]{1,0:T(8,128)} %carried_hbm.1, f32[8,512]{1,0:T(8,128)} %inducing.1, ...), custom_call_target="tpu_custom_call" | custom-call | tf_op jit(solution)/shard_map/substitute/pallas_call | solution.py:370
  105.1 2.0 %finish.1 = (bf16[512,256]{1,0:T(8,128)(2,1)}, f32[128,1024]{1,0:T(8,128)}) custom-call(bf16[256,512]{1,0:T(8,128)(2,1)} %get-tuple-element.4.solved_t, bf16[128,1024]{1,0:T(8,128)(2,1)} %get-tuple-element.5.gram), custom_call_target="tpu_custom_call" | custom-call | tf_op jit(solution)/shard_map/finish/pallas_call | solution.py:354
